TPU v7x, 32 devices: a whole 2x2x4 slice. The times are simulated.
32 devices in a mesh: clus: 8 (over z, core), sub: 4 (over y, x).
Axes of the slice: x: 2, y: 2, z: 4, core: 2. Of those that a mesh axis runs over, the one named last changes fastest.
Arguments:
- right_side: float32 [8, 4, 896, 512], P('clus', 'sub'), may hold values from -6 to 6
- dual_operator: float32 [8, 4, 896, 896], P('clus', 'sub'), may hold values from -1 to 3
- corner_basis: float32 [8, 4, 24, 896], P('clus', 'sub'), may hold values from -0.1875 to 0.1875
- coarse_inverse: float32 [8, 96, 96], P('clus'), may hold values from -1 to 2
- corner_map: int32 [8, 96], P('clus'), may hold values from 0 to 95, each once within a row
- iface_counts: int32 [8, 4, 4], P('clus', 'sub'), may hold values from 0 to 16, as said below
Outputs:
- solution: float32 [8, 4, 896, 512], P('clus', 'sub')
- residual: float32 [8, 4, 896, 512], P('clus', 'sub')
Inputs may be any that keep to these rules, and one draw needn't show every extreme that they name: `iface_counts`: symmetric in its last two dimensions with a zero diagonal; in every cluster one subdomain shares exactly 16 multipliers with every other subdomain of the cluster.
All inputs are finite; a program needn't handle non-finite values.
Results may differ from a plain program's by a relative error of at most 0.00011.
Values sent between devices are 32-bit elements; how exact they have to be, the bound alone decides.
A program may use at most 64 MiB of HBM per device.

v0:
```python
import functools

import jax
import jax.numpy as jnp
from jax import lax
from jax.experimental import pallas as pl
from jax.experimental.pallas import tpu as pltpu
from jax.sharding import PartitionSpec as P

XC = 128
CAP = 16
ITERS = 3
CHUNKS = 2
VMEM_BYTES = 67043328

spectrum_low = 0.5
spectrum_high = 3.0
center_value = (spectrum_high + spectrum_low) / 2.0
half_width = (spectrum_high - spectrum_low) / 2.0
sigma_one = center_value / half_width

MESH = pl.DeviceIdType.MESH
F32 = jnp.float32
BF16 = jnp.bfloat16


def coefficients():
    ratio_now = 1.0 / sigma_one
    pairs = []
    for _ in range(ITERS - 1):
        ratio_next = 1.0 / (2.0 * sigma_one - ratio_now)
        pairs.append((ratio_next * ratio_now, 2.0 * ratio_next / half_width))
        ratio_now = ratio_next
    return pairs


def round_up(value, multiple):
    return -(-value // multiple) * multiple


def exact_dot(a, b, contract=(1, 0)):
    return lax.dot_general(
        a,
        b,
        (((contract[0],), (contract[1],)), ((), ())),
        precision=lax.Precision.HIGHEST,
        preferred_element_type=F32,
    )


def split(value):
    high = value.astype(BF16)
    return high, (value - high.astype(F32)).astype(BF16)


def kernel(
    nclus,
    nsub,
    rhs_hbm,
    op_hbm,
    basis_hbm,
    inv_hbm,
    map_hbm,
    counts_hbm,
    sol_ref,
    res_ref,
    op,
    basis_ref,
    inv_ref,
    map_ref,
    counts_ref,
    x3,
    y3,
    direction,
    back_mat,
    basis_pad,
    sub_send,
    sub_recv,
    face_send,
    face_recv,
    load_sem,
    sub_send_sem,
    sub_recv_sem,
    face_send_sem,
    face_recv_sem,
):
    loc, ncols = rhs_hbm.shape
    ncor = basis_hbm.shape[0]
    coarse = inv_hbm.shape[0]
    per = CAP + ncor
    nsend = nsub * per
    width = ncols // CHUNKS
    edge = 2 * XC
    first = edge + round_up((nsub - 1) * CAP, 128)
    clus = lax.axis_index("clus")
    sub = lax.axis_index("sub")

    barrier = pltpu.get_barrier_semaphore()
    for offset in range(1, nsub):
        pl.semaphore_signal(
            barrier, inc=1, device_id=(clus, lax.rem(sub + offset, nsub)), device_id_type=MESH
        )

    @pl.when(clus > 0)
    def _():
        pl.semaphore_signal(barrier, inc=1, device_id=(clus - 1, sub), device_id_type=MESH)

    @pl.when(clus < nclus - 1)
    def _():
        pl.semaphore_signal(barrier, inc=1, device_id=(clus + 1, sub), device_id_type=MESH)

    small = [
        pltpu.make_async_copy(source, target, load_sem.at[3 + i])
        for i, (source, target) in enumerate(
            (
                (map_hbm, map_ref),
                (inv_hbm, inv_ref),
                (counts_hbm, counts_ref),
                (basis_hbm, basis_ref),
            )
        )
    ]
    for copy in small:
        copy.start()
    load_top = pltpu.make_async_copy(op_hbm.at[0:first], op.at[0:first], load_sem.at[0])
    load_rhs = pltpu.make_async_copy(rhs_hbm, res_ref, load_sem.at[1])
    load_low = pltpu.make_async_copy(op_hbm.at[first:loc], op.at[first:loc], load_sem.at[2])
    load_top.start()
    load_rhs.start()
    load_low.start()

    @pl.when(clus == 0)
    def _():
        face_recv[:, 0] = jnp.zeros(face_recv.shape[:1] + face_recv.shape[2:], F32)

    @pl.when(clus == nclus - 1)
    def _():
        face_recv[:, 1] = jnp.zeros(face_recv.shape[:1] + face_recv.shape[2:], F32)

    basis_pad[...] = jnp.zeros_like(basis_pad)
    for copy in small:
        copy.wait()
    onehot = jnp.where(
        lax.broadcasted_iota(jnp.int32, (coarse, coarse), 0) == map_ref[...], 1.0, 0.0
    ).astype(F32)
    tables = exact_dot(onehot, exact_dot(inv_ref[...], onehot), (0, 0))
    basis = basis_ref[...]
    basis_pad[pl.ds(pl.multiple_of(sub * ncor, 8), ncor), :] = basis
    t_high, t_low = split(tables)
    p_high, p_low = split(basis_pad[...])
    corner_rows = (
        jnp.dot(t_high, p_high, preferred_element_type=F32)
        + jnp.dot(t_high, p_low, preferred_element_type=F32)
        + jnp.dot(t_low, p_high, preferred_element_type=F32)
    )

    nface = nsub * CAP
    slot_row = lax.broadcasted_iota(jnp.int32, (nface, loc), 0)
    place = lax.broadcasted_iota(jnp.int32, (nface, loc), 1) - edge
    inside = slot_row % CAP
    owner = slot_row // CAP
    begin = jnp.int32(0)
    picked = jnp.zeros((nface, loc), F32)
    for p in range(nsub):
        count = counts_ref[0, p]
        hit = (owner == p) & (inside < count) & (place == inside + begin)
        picked = jnp.where(hit, 1.0, picked)
        begin = begin + count
    pad = back_mat.shape[1] - 3 * ncor - 2 * nface

    def build_back():
        b_high, b_low = split(basis)
        stacked = [b_high.astype(F32), b_high.astype(F32), b_low.astype(F32), -picked, -picked]
        if pad:
            stacked.append(jnp.zeros((pad, loc), F32))
        back_mat[...] = jnp.transpose(jnp.concatenate(stacked, axis=0)).astype(BF16)

    def put_split(begin_row, high, low):
        rows = high.shape[0]
        x3[begin_row : begin_row + rows, 0:loc] = high
        x3[begin_row : begin_row + rows, loc : 2 * loc] = high
        x3[begin_row : begin_row + rows, 2 * loc : 3 * loc] = low

    def put_rows(begin_row, value):
        put_split(begin_row, *split(value))

    def put_direction(columns, value):
        high, low = split(value)
        y3[0:loc, columns] = high
        y3[loc : 2 * loc, columns] = low
        y3[2 * loc : 3 * loc, columns] = high

    put_rows(nface, corner_rows)
    load_top.wait()
    put_rows(nsend, op[0:edge])
    chosen = picked[:, edge:first].astype(BF16)
    m_high, m_low = split(op[edge:first])
    put_split(
        0,
        jnp.dot(chosen, m_high, preferred_element_type=F32).astype(BF16),
        jnp.dot(chosen, m_low, preferred_element_type=F32).astype(BF16),
    )
    load_rhs.wait()
    for c in range(CHUNKS):
        columns = slice(c * width, (c + 1) * width)
        start = res_ref[:, columns] / center_value
        direction[:, columns] = start
        sol_ref[:, columns] = start
        put_direction(columns, start)

    near = jnp.where(clus > 0, 1, 0) + jnp.where(clus < nclus - 1, 1, 0)
    pl.semaphore_wait(barrier, nsub - 1 + near)

    def sub_copy(slot, offset):
        partner = lax.rem(sub + offset, nsub)
        return pltpu.make_async_remote_copy(
            src_ref=sub_send.at[slot, partner],
            dst_ref=sub_recv.at[slot, sub],
            send_sem=sub_send_sem.at[slot, offset - 1],
            recv_sem=sub_recv_sem.at[slot, offset - 1],
            device_id=(clus, partner),
            device_id_type=MESH,
        )

    def face_copy(slot, side):
        return pltpu.make_async_remote_copy(
            src_ref=face_send.at[slot, side],
            dst_ref=face_recv.at[slot, side],
            send_sem=face_send_sem.at[slot, side],
            recv_sem=face_recv_sem.at[slot, side],
            device_id=(clus + (1 if side == 0 else -1), sub),
            device_id_type=MESH,
        )

    def send_part(iteration, c):
        columns = slice(c * width, (c + 1) * width)
        slot = iteration * CHUNKS + c
        head = jnp.dot(x3[0:nsend, :], y3[:, columns], preferred_element_type=F32)
        for p in range(nsub):
            sub_send[slot, p, 0:CAP] = head[p * CAP : (p + 1) * CAP]
            sub_send[slot, p, CAP:per] = head[nface + p * ncor : nface + (p + 1) * ncor]
        for offset in range(1, nsub):
            sub_copy(slot, offset).start()
        faces = jnp.dot(
            x3[nsend : nsend + edge, :], y3[:, columns], preferred_element_type=F32
        )
        face_send[slot, 0] = faces[XC:edge]
        face_send[slot, 1] = faces[0:XC]

        @pl.when(clus < nclus - 1)
        def _():
            face_copy(slot, 0).start()

        @pl.when(clus > 0)
        def _():
            face_copy(slot, 1).start()

        sub_recv[slot, pl.ds(sub, 1)] = sub_send[slot, pl.ds(sub, 1)]
        res_ref[0:edge, columns] = res_ref[0:edge, columns] - faces

    def rest_part():
        tail = jnp.dot(x3[nsend + edge :, :], y3[...], preferred_element_type=F32)
        res_ref[edge:, :] = res_ref[edge:, :] - tail

    def receive_part(iteration, c):
        columns = slice(c * width, (c + 1) * width)
        slot = iteration * CHUNKS + c
        for offset in range(1, nsub):
            sub_copy(slot, offset).wait_recv()

        @pl.when(clus > 0)
        def _():
            face_copy(slot, 0).wait_recv()

        @pl.when(clus < nclus - 1)
        def _():
            face_copy(slot, 1).wait_recv()

        back = sub_recv[slot, 0, CAP:per]
        for p in range(1, nsub):
            back = back + sub_recv[slot, p, CAP:per]
        faces = jnp.concatenate([sub_recv[slot, p, 0:CAP] for p in range(nsub)], axis=0)
        k_high, k_low = [part.astype(F32) for part in split(back)]
        f_high, f_low = [part.astype(F32) for part in split(faces)]
        gathered = [k_high, k_low, k_high, f_high, f_low]
        if pad:
            gathered.append(jnp.zeros((pad, width), F32))
        operand = jnp.concatenate(gathered, axis=0).astype(BF16)
        fix = jnp.dot(back_mat[...], operand, preferred_element_type=F32)
        across = face_recv[slot].reshape(edge, width)
        top = res_ref[0:edge, columns] - fix[0:edge] + across
        low = res_ref[edge:, columns] - fix[edge:]
        value = jnp.concatenate([top, low], axis=0)
        res_ref[:, columns] = value
        if iteration + 1 < ITERS:
            keep, gain = coefficients()[iteration]
            moved = keep * direction[:, columns] + gain * value
            direction[:, columns] = moved
            sol_ref[:, columns] = sol_ref[:, columns] + moved
            put_direction(columns, moved)

    for iteration in range(ITERS):
        for c in range(CHUNKS):
            if iteration:
                receive_part(iteration - 1, c)
            send_part(iteration, c)
        if iteration == 0:
            load_low.wait()
            put_rows(nsend + edge, op[edge:loc])
            build_back()
        rest_part()
    for c in range(CHUNKS):
        receive_part(ITERS - 1, c)

    for slot in range(ITERS * CHUNKS):
        for offset in range(1, nsub):
            sub_copy(slot, offset).wait_send()

        @pl.when(clus < nclus - 1)
        def _():
            face_copy(slot, 0).wait_send()

        @pl.when(clus > 0)
        def _():
            face_copy(slot, 1).wait_send()


def flush(sol_vmem, res_vmem, sol_hbm, res_hbm, sem):
    first = pltpu.make_async_copy(sol_vmem, sol_hbm, sem.at[0])
    second = pltpu.make_async_copy(res_vmem, res_hbm, sem.at[1])
    first.start()
    second.start()
    first.wait()
    second.wait()


def on_device(right_side, dual_operator, corner_basis, coarse_inverse, corner_map, iface_counts):
    nsub = lax.axis_size("sub")
    nclus = lax.axis_size("clus")
    loc, ncols = right_side.shape[2:]
    ncor = corner_basis.shape[2]
    per = CAP + ncor
    slots = ITERS * CHUNKS
    width = ncols // CHUNKS
    rows = nsub * per + loc
    depth = round_up(3 * ncor + 2 * nsub * CAP, 128)
    vmem = pl.BlockSpec(memory_space=pltpu.VMEM)
    hbm = pl.BlockSpec(memory_space=pltpu.HBM)
    shape = jax.ShapeDtypeStruct((loc, ncols), F32)
    dma = pltpu.SemaphoreType.DMA
    outs = pl.pallas_call(
        functools.partial(kernel, nclus, nsub),
        out_shape=(pltpu.VMEM(shape.shape, F32), pltpu.VMEM(shape.shape, F32)),
        in_specs=[hbm] * 6,
        out_specs=(vmem, vmem),
        scratch_shapes=[
            pltpu.VMEM((loc, loc), F32),
            pltpu.VMEM((ncor, loc), F32),
            pltpu.VMEM(coarse_inverse.shape[1:], F32),
            pltpu.VMEM(corner_map.shape, jnp.int32),
            pltpu.SMEM(iface_counts.shape[1:], jnp.int32),
            pltpu.VMEM((rows, 3 * loc), BF16),
            pltpu.VMEM((3 * loc, ncols), BF16),
            pltpu.VMEM((loc, ncols), F32),
            pltpu.VMEM((loc, depth), BF16),
            pltpu.VMEM((nsub * ncor, loc), F32),
            pltpu.VMEM((slots, nsub, per, width), F32),
            pltpu.VMEM((slots, nsub, per, width), F32),
            pltpu.VMEM((slots, 2, XC, width), F32),
            pltpu.VMEM((slots, 2, XC, width), F32),
            dma((7,)),
            dma((slots, nsub - 1)),
            dma((slots, nsub - 1)),
            dma((slots, 2)),
            dma((slots, 2)),
        ],
        compiler_params=pltpu.CompilerParams(
            collective_id=0, has_side_effects=True, vmem_limit_bytes=VMEM_BYTES - 2 * loc * ncols * 4 - 32 * 1024
        ),
    )(
        right_side[0, 0],
        dual_operator[0, 0],
        corner_basis[0, 0],
        coarse_inverse[0],
        corner_map,
        iface_counts[0],
    )
    outs = pl.pallas_call(
        flush,
        out_shape=(shape, shape),
        in_specs=[pl.BlockSpec(memory_space=pl.ANY)] * 2,
        out_specs=(hbm, hbm),
        scratch_shapes=[dma((2,))],
        compiler_params=pltpu.CompilerParams(vmem_limit_bytes=4 * 1024 * 1024),
    )(*outs)
    return outs[0][None, None], outs[1][None, None]


def solution(mesh):
    placed = (
        P("clus", "sub", None, None),
        P("clus", "sub", None, None),
        P("clus", "sub", None, None),
        P("clus", None, None),
        P("clus", None),
        P("clus", "sub", None),
    )
    return jax.shard_map(
        on_device,
        mesh=mesh,
        in_specs=placed,
        out_specs=(P("clus", "sub", None, None), P("clus", "sub", None, None)),
        check_vma=False,
    )
```

profile of v0, /device:TPU:0, one launch (start us, length us, event | category | flops | bytes accessed | tf_op | source)
XLA Modules:
  0.0 26.6 jit_solution(16513238705921169327)
XLA Ops:
  0.6 24.1 %shard_map.77 = (f32[896,512]{1,0:T(8,128)S(1)}, f32[896,512]{1,0:T(8,128)S(1)}) custom-call(f32[896,512]{1,0:T(8,128)} %bitcast.8, f32[896,896]{1,0:T(8,128)} %bitcast.7, f32[24,896]{1,0:T(8,128)} %bitcast.9, f32[96,96]{1,0:T(8,128)} %bitcast.10, s32[1,96]{1,0:T(1,128)} %map_hbm.1, s32[1,4]{1,0:T(1,128)} %bitcast.11), custom_call_target="tpu_custom_call" | custom-call | tf_op jit(solution)/shard_map/pallas_call | solution.py:351
  24.7 1.9 %shard_map.78 = (f32[896,512]{1,0:T(8,128)}, f32[896,512]{1,0:T(8,128)}) custom-call(f32[896,512]{1,0:T(8,128)S(1)} %get-tuple-element.6.sol_vmem, f32[896,512]{1,0:T(8,128)S(1)} %get-tuple-element.7.res_vmem), custom_call_target="tpu_custom_call" | custom-call | tf_op jit(solution)/shard_map/pallas_call | solution.py:388
where the time goes:
time: 26.8 us; the launch traced here: 26.6 us
  Pallas kernels  26 us (97%)
  between operations  0.64 us (2%)
    pallas_call x1, Pallas kernels, on_device(): pl.pallas_call(functools.partial(kernel, nclus, nsub), out_shape=(pltpu.V...  24.1 us
    pallas_call x1, Pallas kernels, on_device(): pl.pallas_call(flush, out_shape=(shape, shape), in_specs=[pl.BlockSpec(me...  1.85 us

commit v1 on v0

--- a/solution.py
+++ b/solution.py
@@ -11,6 +11,7 @@
 CAP = 16
 ITERS = 3
 CHUNKS = 2
+BLOCK = 320
 VMEM_BYTES = 67043328
 
 spectrum_low = 0.5
@@ -36,16 +37,6 @@
 
 def round_up(value, multiple):
     return -(-value // multiple) * multiple
-
-
-def exact_dot(a, b, contract=(1, 0)):
-    return lax.dot_general(
-        a,
-        b,
-        (((contract[0],), (contract[1],)), ((), ())),
-        precision=lax.Precision.HIGHEST,
-        preferred_element_type=F32,
-    )
 
 
 def split(value):
@@ -69,9 +60,12 @@
     inv_ref,
     map_ref,
     counts_ref,
-    x3,
-    y3,
-    direction,
+    x_high,
+    x_low,
+    y_high,
+    y_low,
+    ahead,
+    fixes,
     back_mat,
     basis_pad,
     sub_send,
@@ -110,7 +104,7 @@
         pl.semaphore_signal(barrier, inc=1, device_id=(clus + 1, sub), device_id_type=MESH)
 
     small = [
-        pltpu.make_async_copy(source, target, load_sem.at[3 + i])
+        pltpu.make_async_copy(source, target, load_sem.at[2 + CHUNKS + i])
         for i, (source, target) in enumerate(
             (
                 (map_hbm, map_ref),
@@ -122,11 +116,17 @@
     ]
     for copy in small:
         copy.start()
+    spans = [slice(c * width, (c + 1) * width) for c in range(CHUNKS)]
     load_top = pltpu.make_async_copy(op_hbm.at[0:first], op.at[0:first], load_sem.at[0])
-    load_rhs = pltpu.make_async_copy(rhs_hbm, res_ref, load_sem.at[1])
-    load_low = pltpu.make_async_copy(op_hbm.at[first:loc], op.at[first:loc], load_sem.at[2])
+    load_low = pltpu.make_async_copy(op_hbm.at[first:loc], op.at[first:loc], load_sem.at[1])
+    load_rhs = [
+        pltpu.make_async_copy(rhs_hbm.at[:, span], res_ref.at[:, span], load_sem.at[2 + c])
+        for c, span in enumerate(spans)
+    ]
+    load_rhs[0].start()
     load_top.start()
-    load_rhs.start()
+    for copy in load_rhs[1:]:
+        copy.start()
     load_low.start()
 
     @pl.when(clus == 0)
@@ -142,11 +142,19 @@
         copy.wait()
     onehot = jnp.where(
         lax.broadcasted_iota(jnp.int32, (coarse, coarse), 0) == map_ref[...], 1.0, 0.0
-    ).astype(F32)
-    tables = exact_dot(onehot, exact_dot(inv_ref[...], onehot), (0, 0))
+    ).astype(BF16)
+    chosen_columns = [
+        jnp.dot(part, onehot, preferred_element_type=F32).astype(BF16)
+        for part in split(inv_ref[...])
+    ]
+    t_high, t_low = [
+        lax.dot_general(
+            onehot, part, (((0,), (0,)), ((), ())), preferred_element_type=F32
+        ).astype(BF16)
+        for part in chosen_columns
+    ]
     basis = basis_ref[...]
     basis_pad[pl.ds(pl.multiple_of(sub * ncor, 8), ncor), :] = basis
-    t_high, t_low = split(tables)
     p_high, p_low = split(basis_pad[...])
     corner_rows = (
         jnp.dot(t_high, p_high, preferred_element_type=F32)
@@ -155,12 +163,13 @@
     )
 
     nface = nsub * CAP
-    slot_row = lax.broadcasted_iota(jnp.int32, (nface, loc), 0)
-    place = lax.broadcasted_iota(jnp.int32, (nface, loc), 1) - edge
+    reach = first - edge
+    slot_row = lax.broadcasted_iota(jnp.int32, (nface, reach), 0)
+    place = lax.broadcasted_iota(jnp.int32, (nface, reach), 1)
     inside = slot_row % CAP
     owner = slot_row // CAP
     begin = jnp.int32(0)
-    picked = jnp.zeros((nface, loc), F32)
+    picked = jnp.zeros((nface, reach), F32)
     for p in range(nsub):
         count = counts_ref[0, p]
         hit = (owner == p) & (inside < count) & (place == inside + begin)
@@ -170,43 +179,57 @@
 
     def build_back():
         b_high, b_low = split(basis)
-        stacked = [b_high.astype(F32), b_high.astype(F32), b_low.astype(F32), -picked, -picked]
+        spread = jnp.concatenate(
+            [
+                jnp.zeros((nface, edge), F32),
+                -picked,
+                jnp.zeros((nface, loc - first), F32),
+            ],
+            axis=1,
+        )
+        stacked = [b_high.astype(F32), b_high.astype(F32), b_low.astype(F32), spread, spread]
         if pad:
             stacked.append(jnp.zeros((pad, loc), F32))
         back_mat[...] = jnp.transpose(jnp.concatenate(stacked, axis=0)).astype(BF16)
 
     def put_split(begin_row, high, low):
         rows = high.shape[0]
-        x3[begin_row : begin_row + rows, 0:loc] = high
-        x3[begin_row : begin_row + rows, loc : 2 * loc] = high
-        x3[begin_row : begin_row + rows, 2 * loc : 3 * loc] = low
+        x_high[begin_row : begin_row + rows, :] = high
+        x_low[begin_row : begin_row + rows, :] = low
 
     def put_rows(begin_row, value):
         put_split(begin_row, *split(value))
 
-    def put_direction(columns, value):
+    def put_direction(columns, value, begin_row, end_row):
         high, low = split(value)
-        y3[0:loc, columns] = high
-        y3[loc : 2 * loc, columns] = low
-        y3[2 * loc : 3 * loc, columns] = high
+        y_high[begin_row:end_row, columns] = high
+        y_low[begin_row:end_row, columns] = low
+
+    def times(begin_row, end_row, columns):
+        high = x_high[begin_row:end_row, :]
+        rows = jnp.concatenate([high, high, x_low[begin_row:end_row, :]], axis=1)
+        top = y_high[:, columns]
+        deep = jnp.concatenate([top, y_low[:, columns], top], axis=0)
+        return jnp.dot(rows, deep, preferred_element_type=F32)
+
+    def begin_part(c):
+        load_rhs[c].wait()
+        put_direction(spans[c], res_ref[:, spans[c]] * (1.0 / center_value), 0, loc)
 
     put_rows(nface, corner_rows)
+    begin_part(0)
     load_top.wait()
     put_rows(nsend, op[0:edge])
-    chosen = picked[:, edge:first].astype(BF16)
+    chosen = picked.astype(BF16)
     m_high, m_low = split(op[edge:first])
     put_split(
         0,
         jnp.dot(chosen, m_high, preferred_element_type=F32).astype(BF16),
         jnp.dot(chosen, m_low, preferred_element_type=F32).astype(BF16),
     )
-    load_rhs.wait()
-    for c in range(CHUNKS):
-        columns = slice(c * width, (c + 1) * width)
-        start = res_ref[:, columns] / center_value
-        direction[:, columns] = start
-        sol_ref[:, columns] = start
-        put_direction(columns, start)
+
+    for c in range(1, CHUNKS):
+        begin_part(c)
 
     near = jnp.where(clus > 0, 1, 0) + jnp.where(clus < nclus - 1, 1, 0)
     pl.semaphore_wait(barrier, nsub - 1 + near)
@@ -233,19 +256,17 @@
         )
 
     def send_part(iteration, c):
-        columns = slice(c * width, (c + 1) * width)
+        columns = spans[c]
         slot = iteration * CHUNKS + c
-        head = jnp.dot(x3[0:nsend, :], y3[:, columns], preferred_element_type=F32)
+        middle = (nsend + edge) // 2
+        lead = jnp.concatenate([times(0, middle, columns), times(middle, nsend + edge, columns)], axis=0)
         for p in range(nsub):
-            sub_send[slot, p, 0:CAP] = head[p * CAP : (p + 1) * CAP]
-            sub_send[slot, p, CAP:per] = head[nface + p * ncor : nface + (p + 1) * ncor]
+            sub_send[slot, p, 0:CAP] = lead[p * CAP : (p + 1) * CAP]
+            sub_send[slot, p, CAP:per] = lead[nface + p * ncor : nface + (p + 1) * ncor]
+        face_send[slot, 0] = lead[nsend + XC : nsend + edge]
+        face_send[slot, 1] = lead[nsend : nsend + XC]
         for offset in range(1, nsub):
             sub_copy(slot, offset).start()
-        faces = jnp.dot(
-            x3[nsend : nsend + edge, :], y3[:, columns], preferred_element_type=F32
-        )
-        face_send[slot, 0] = faces[XC:edge]
-        face_send[slot, 1] = faces[0:XC]
 
         @pl.when(clus < nclus - 1)
         def _():
@@ -255,15 +276,36 @@
         def _():
             face_copy(slot, 1).start()
 
-        sub_recv[slot, pl.ds(sub, 1)] = sub_send[slot, pl.ds(sub, 1)]
-        res_ref[0:edge, columns] = res_ref[0:edge, columns] - faces
-
-    def rest_part():
-        tail = jnp.dot(x3[nsend + edge :, :], y3[...], preferred_element_type=F32)
-        res_ref[edge:, :] = res_ref[edge:, :] - tail
+    def advance(iteration, c, begin_row, end_row, product):
+        rows = slice(begin_row, end_row)
+        columns = spans[c]
+        value = res_ref[rows, columns]
+        if iteration == 0:
+            moved = value * (1.0 / center_value)
+            sol_ref[rows, columns] = moved
+        else:
+            fix = fixes[rows, columns]
+            value = value - fix
+            moved = ahead[rows, columns] - coefficients()[iteration - 1][1] * fix
+            sol_ref[rows, columns] = sol_ref[rows, columns] + moved
+        value = value - product
+        res_ref[rows, columns] = value
+        if iteration + 1 < ITERS:
+            keep, gain = coefficients()[iteration]
+            ahead[rows, columns] = keep * moved + gain * value
+
+    def rest_part(iteration):
+        tail = times(nsend + edge, nsend + loc, slice(0, ncols))
+        for c in range(CHUNKS):
+            slot = iteration * CHUNKS + c
+            sub_recv[slot, pl.ds(sub, 1)] = sub_send[slot, pl.ds(sub, 1)]
+            advance(iteration, c, 0, XC, face_send[slot, 1])
+            advance(iteration, c, XC, edge, face_send[slot, 0])
+        for c in range(CHUNKS):
+            advance(iteration, c, edge, loc, tail[:, spans[c]])
 
     def receive_part(iteration, c):
-        columns = slice(c * width, (c + 1) * width)
+        columns = spans[c]
         slot = iteration * CHUNKS + c
         for offset in range(1, nsub):
             sub_copy(slot, offset).wait_recv()
@@ -286,18 +328,18 @@
         if pad:
             gathered.append(jnp.zeros((pad, width), F32))
         operand = jnp.concatenate(gathered, axis=0).astype(BF16)
-        fix = jnp.dot(back_mat[...], operand, preferred_element_type=F32)
         across = face_recv[slot].reshape(edge, width)
-        top = res_ref[0:edge, columns] - fix[0:edge] + across
-        low = res_ref[edge:, columns] - fix[edge:]
-        value = jnp.concatenate([top, low], axis=0)
-        res_ref[:, columns] = value
-        if iteration + 1 < ITERS:
-            keep, gain = coefficients()[iteration]
-            moved = keep * direction[:, columns] + gain * value
-            direction[:, columns] = moved
-            sol_ref[:, columns] = sol_ref[:, columns] + moved
-            put_direction(columns, moved)
+        bounds = [0, edge] + list(range(edge + BLOCK, loc, BLOCK)) + [loc]
+        for low, high in zip(bounds[:-1], bounds[1:]):
+            fix = jnp.dot(back_mat[low:high, :], operand, preferred_element_type=F32)
+            if low == 0:
+                fix = fix - across
+            if iteration + 1 < ITERS:
+                fixes[low:high, columns] = fix
+                moved = ahead[low:high, columns] - coefficients()[iteration][1] * fix
+                put_direction(columns, moved, low, high)
+            else:
+                res_ref[low:high, columns] = res_ref[low:high, columns] - fix
 
     for iteration in range(ITERS):
         for c in range(CHUNKS):
@@ -308,7 +350,7 @@
             load_low.wait()
             put_rows(nsend + edge, op[edge:loc])
             build_back()
-        rest_part()
+        rest_part(iteration)
     for c in range(CHUNKS):
         receive_part(ITERS - 1, c)
 
@@ -359,8 +401,11 @@
             pltpu.VMEM(coarse_inverse.shape[1:], F32),
             pltpu.VMEM(corner_map.shape, jnp.int32),
             pltpu.SMEM(iface_counts.shape[1:], jnp.int32),
-            pltpu.VMEM((rows, 3 * loc), BF16),
-            pltpu.VMEM((3 * loc, ncols), BF16),
+            pltpu.VMEM((rows, loc), BF16),
+            pltpu.VMEM((rows, loc), BF16),
+            pltpu.VMEM((loc, ncols), BF16),
+            pltpu.VMEM((loc, ncols), BF16),
+            pltpu.VMEM((loc, ncols), F32),
             pltpu.VMEM((loc, ncols), F32),
             pltpu.VMEM((loc, depth), BF16),
             pltpu.VMEM((nsub * ncor, loc), F32),
@@ -368,7 +413,7 @@
             pltpu.VMEM((slots, nsub, per, width), F32),
             pltpu.VMEM((slots, 2, XC, width), F32),
             pltpu.VMEM((slots, 2, XC, width), F32),
-            dma((7,)),
+            dma((6 + CHUNKS,)),
             dma((slots, nsub - 1)),
             dma((slots, nsub - 1)),
             dma((slots, 2)),

time: 26.8 us -> 25.7 us (0.959)
  Pallas kernels: 26 us -> 24.9 us
    pallas_call x1, Pallas kernels: 24.1 us -> 23.1 us  [on_device(): pl.pallas_call(functools.partial(kernel, nclus, nsub), out_shape=(pltpu.V...]
where the time goes in v1:
time: 25.7 us; the launch traced here: 25.5 us
  Pallas kernels  24.9 us (97%)
  between operations  0.64 us (2%)
    pallas_call x1, Pallas kernels, on_device(): pl.pallas_call(functools.partial(kernel, nclus, nsub), out_shape=(pltpu.V...  23.1 us
    pallas_call x1, Pallas kernels, on_device(): pl.pallas_call(flush, out_shape=(shape, shape), in_specs=[pl.BlockSpec(me...  1.85 us

profile of v1, /device:TPU:0, one launch (start us, length us, event | category | flops | bytes accessed | tf_op | source)
XLA Modules:
  0.0 25.5 jit_solution(5561821891750879703)
XLA Ops:
  0.6 23.1 %shard_map.77 = (f32[896,512]{1,0:T(8,128)S(1)}, f32[896,512]{1,0:T(8,128)S(1)}) custom-call(f32[896,512]{1,0:T(8,128)} %bitcast.8, f32[896,896]{1,0:T(8,128)} %bitcast.7, f32[24,896]{1,0:T(8,128)} %bitcast.9, f32[96,96]{1,0:T(8,128)} %bitcast.10, s32[1,96]{1,0:T(1,128)} %map_hbm.1, s32[1,4]{1,0:T(1,128)} %bitcast.11), custom_call_target="tpu_custom_call" | custom-call | tf_op jit(solution)/shard_map/pallas_call | solution.py:393
  23.7 1.9 %shard_map.78 = (f32[896,512]{1,0:T(8,128)}, f32[896,512]{1,0:T(8,128)}) custom-call(f32[896,512]{1,0:T(8,128)S(1)} %get-tuple-element.6.sol_vmem, f32[896,512]{1,0:T(8,128)S(1)} %get-tuple-element.7.res_vmem), custom_call_target="tpu_custom_call" | custom-call | tf_op jit(solution)/shard_map/pallas_call | solution.py:433

commit v2 on v1

--- a/solution.py
+++ b/solution.py
@@ -228,9 +228,6 @@
         jnp.dot(chosen, m_low, preferred_element_type=F32).astype(BF16),
     )
 
-    for c in range(1, CHUNKS):
-        begin_part(c)
-
     near = jnp.where(clus > 0, 1, 0) + jnp.where(clus < nclus - 1, 1, 0)
     pl.semaphore_wait(barrier, nsub - 1 + near)
 
@@ -345,6 +342,8 @@
         for c in range(CHUNKS):
             if iteration:
                 receive_part(iteration - 1, c)
+            elif c:
+                begin_part(c)
             send_part(iteration, c)
         if iteration == 0:
             load_low.wait()

time: 25.7 us -> 25.5 us (level)
  no operation moved by 1% of the time
where the time goes in v2:
time: 25.5 us; the launch traced here: 25.3 us
  Pallas kernels  24.7 us (97%)
  between operations  0.64 us (3%)
    pallas_call x1, Pallas kernels, on_device(): pl.pallas_call(functools.partial(kernel, nclus, nsub), out_shape=(pltpu.V...  22.8 us
    pallas_call x1, Pallas kernels, on_device(): pl.pallas_call(flush, out_shape=(shape, shape), in_specs=[pl.BlockSpec(me...  1.85 us

profile of v2, /device:TPU:0, one launch (start us, length us, event | category | flops | bytes accessed | tf_op | source)
XLA Modules:
  0.0 25.3 jit_solution(9378977328189656166)
XLA Ops:
  0.6 22.8 %shard_map.77 = (f32[896,512]{1,0:T(8,128)S(1)}, f32[896,512]{1,0:T(8,128)S(1)}) custom-call(f32[896,512]{1,0:T(8,128)} %bitcast.8, f32[896,896]{1,0:T(8,128)} %bitcast.7, f32[24,896]{1,0:T(8,128)} %bitcast.9, f32[96,96]{1,0:T(8,128)} %bitcast.10, s32[1,96]{1,0:T(1,128)} %map_hbm.1, s32[1,4]{1,0:T(1,128)} %bitcast.11), custom_call_target="tpu_custom_call" | custom-call | tf_op jit(solution)/shard_map/pallas_call | solution.py:392
  23.5 1.9 %shard_map.78 = (f32[896,512]{1,0:T(8,128)}, f32[896,512]{1,0:T(8,128)}) custom-call(f32[896,512]{1,0:T(8,128)S(1)} %get-tuple-element.6.sol_vmem, f32[896,512]{1,0:T(8,128)S(1)} %get-tuple-element.7.res_vmem), custom_call_target="tpu_custom_call" | custom-call | tf_op jit(solution)/shard_map/pallas_call | solution.py:432
